TPU v7x, 128 devices: a whole 4x4x4 slice. The times are simulated.
128 devices in a mesh: grp: 8 (over y, core), mig: 4 (over x), pen: 4 (over z).
Axes of the slice: x: 4, y: 4, z: 4, core: 2. Of those that a mesh axis runs over, the one named last changes fastest.
Arguments:
- fields: float32 [4096, 9, 4096], P(('grp', 'mig', 'pen')), may hold values from -6 to 6
- ghosts: float32 [4096, 9, 1536], P(('grp', 'mig', 'pen')), may hold values from -6 to 6
- velocity: float32 [3, 4096], P(None, ('grp', 'mig', 'pen')), may hold values from -1 to 1
- rate_matrix: float32 [9, 9], replicated, may hold values from -2 to 2
- recent_tend: bfloat16 [4096, 9, 4096], P(('grp', 'mig', 'pen')), may hold values from -6 to 6
- older_tend: bfloat16 [4096, 9, 4096], P(('grp', 'mig', 'pen')), may hold values from -6 to 6
- destination: int32 [4096], P(('grp', 'mig', 'pen')), may hold values from 0 to 15, as said below
- target_slot: int32 [4096], P(('grp', 'mig', 'pen')), may hold values from 0 to 32, as said below
- live_counts: int32 [128], P(('grp', 'mig', 'pen')), may hold values from 0 to 32, as said below
- tile_ids: int32 [4096], P(('grp', 'mig', 'pen')), may hold values from 0 to 4095, each once
- sensor: float32 [128, 131072], P('pen', ('grp', 'mig')), may hold values from 0 to 4
- flame_flags: int32 [8, 512], P('pen', ('grp', 'mig')), may hold values 0 or 1
Outputs:
- new_fields: float32 [4096, 9, 4096], P(('grp', 'mig', 'pen'))
- new_tend: bfloat16 [4096, 9, 4096], P(('grp', 'mig', 'pen'))
- filtered: float32 [128, 131072], P('pen', ('grp', 'mig'))
Inputs may be any that keep to these rules, and one draw needn't show every extreme that they name: `destination`: index (mig-major) within the old slot's group of devices sharing its grp index; a device names every other device of its group for at most one of its slots; slots whose tile stays, and slots without a tile, name the device itself. `target_slot`: 32 marks an old slot without a tile; at each device the kept and arriving tiles take the slots 0 to its live count - 1, each exactly once. `live_counts`: equals the number of tiles that a device keeps or receives.
All inputs are finite; a program needn't handle non-finite values. No bound on the sum of `flame_flags` on one device may be relied on, other than what follows from the above.
Results may differ from a plain program's by a relative error of at most 0.001.
Values may be sent and summed in bfloat16 or wider, within the bound.
A program may use at most 320 MiB of HBM per device.

v0:
```python
import jax
import jax.numpy as jnp
from jax import lax
from jax.sharding import Mesh
from jax.sharding import PartitionSpec as P

TE = 16
TZ = 2
TCOL = 16
GRP_MIG_PEN = ("grp_0", "grp_1", "mig", "pen")
GRP_MIG = ("grp_0", "grp_1", "mig")


viscous = 0.05
step_size = 0.25
thicken = 5.0


def side_by_side(arrays, axis, split_dim, concat_dim, along):
    columns = [a.reshape(*a.shape[:along], -1) for a in arrays]
    both = jnp.concatenate(columns, axis=along)
    result, at, outs = (
        lax.all_to_all(both, axis, split_axis=split_dim, concat_axis=concat_dim, tiled=True),
        0,
        [],
    )
    for a, column in zip(arrays, columns):
        slab = result[..., at : at + column.shape[along]]
        outs.append(slab.reshape(*slab.shape[:along], *a.shape[along:]))
        at += column.shape[along]
    return tuple(outs)


def passed_along(x, axis, by):
    peers = lax.axis_size(axis)
    return lax.ppermute(x, axis, [(i, (i + by) % peers) for i in range(peers)])


def in_order(blocks, dim):
    blocks = jnp.moveaxis(blocks, 0, dim)
    shape = blocks.shape
    return blocks.reshape(*shape[:dim], shape[dim] * shape[dim + 1], *shape[dim + 2 :])


def all_blocks(x, axes, order):
    blocks = x
    for k in order:
        blocks = lax.all_gather(blocks, axes[k])
    done = order[::-1]
    back = [done.index(k) for k in range(len(axes))]
    blocks = blocks.transpose(*back, *range(len(axes), blocks.ndim))
    return blocks.reshape(-1, *x.shape)


def whole_of(x, axes, order, dim):
    return in_order(all_blocks(x, axes, order), dim)


def placement(tile_edge, which):
    face_size = tile_edge * tile_edge
    cell_index = jnp.arange(tile_edge**3, dtype=jnp.int32)
    z_index = cell_index % tile_edge
    y_index = cell_index // tile_edge % tile_edge
    x_index = cell_index // face_size
    direction = which // 2
    edge_value = 0 if which % 2 == 0 else tile_edge - 1
    if direction == 0:
        on_face = x_index == edge_value
        face_spot = y_index * tile_edge + z_index
    elif direction == 1:
        on_face = y_index == edge_value
        face_spot = x_index * tile_edge + z_index
    else:
        on_face = z_index == edge_value
        face_spot = x_index * tile_edge + y_index
    face_range = jnp.arange(face_size, dtype=jnp.int32)[:, None]
    return ((face_range == face_spot[None, :]) & on_face[None, :]).astype(jnp.float32)


def tendency(fields, ghosts, velocity, thickening, rate_matrix, tile_edge):
    face_size = tile_edge * tile_edge
    tile_cells = tile_edge**3
    lead = fields.shape[0]
    species = fields.shape[1]
    cell_index = jnp.arange(tile_cells, dtype=jnp.int32)
    z_index = cell_index % tile_edge
    y_index = cell_index // tile_edge % tile_edge
    x_index = cell_index // face_size

    def outside(which):
        face_values = ghosts[:, :, which * face_size : (which + 1) * face_size].reshape(
            lead * species, face_size
        )
        placed = jnp.dot(face_values, placement(tile_edge, which), precision=lax.Precision.HIGHEST)
        return placed.reshape(lead, species, tile_cells)

    def inside(shift, interior):
        return jnp.roll(fields, shift, axis=2) * interior.astype(jnp.float32)

    x_low = inside(face_size, x_index != 0) + outside(0)
    x_high = inside(-face_size, x_index != tile_edge - 1) + outside(1)
    y_low = inside(tile_edge, y_index != 0) + outside(2)
    y_high = inside(-tile_edge, y_index != tile_edge - 1) + outside(3)
    z_low = inside(1, z_index != 0) + outside(4)
    z_high = inside(-1, z_index != tile_edge - 1) + outside(5)
    laplace = x_low + x_high + y_low + y_high + z_low + z_high - 6.0 * fields
    advection = 0.5 * (
        velocity[0][:, None, None] * (x_high - x_low)
        + velocity[1][:, None, None] * (y_high - y_low)
        + velocity[2][:, None, None] * (z_high - z_low)
    )
    burning = fields[:, 0] * fields[:, 1]
    reaction = jnp.einsum(
        "sk,nkc->nsc", rate_matrix, fields * burning[:, None, :], precision=lax.Precision.HIGHEST
    )
    thick_slot = thickening[:, None, None]
    return thick_slot * viscous * laplace - advection + reaction / thick_slot


def gauss_total(reach):
    sigma = reach / 2.0
    offsets = jnp.arange(-reach, reach + 1).astype(jnp.float32)
    return jnp.sum(jnp.exp(-offsets * offsets / (2.0 * sigma * sigma)))


def banded(row_total, reach):
    sigma = reach / 2.0
    row_index = jnp.arange(row_total, dtype=jnp.int32)[:, None]
    col_index = jnp.arange(row_total + 2 * reach, dtype=jnp.int32)[None, :]
    offset = (col_index - reach - row_index).astype(jnp.float32)
    weights = jnp.where(
        jnp.abs(offset) <= reach, jnp.exp(-offset * offset / (2.0 * sigma * sigma)), 0.0
    )
    return weights / gauss_total(reach)


def tile_thickening(filtered, tile_edge, tile_rows, tile_cols):
    clipped = jnp.minimum(filtered, 1.0)
    shaped = clipped.reshape(tile_rows, tile_edge, tile_cols, tile_edge * tile_edge)
    return 1.0 + (thicken - 1.0) * jnp.mean(shaped, axis=(1, 3))


def local(
    fields,
    ghosts,
    velocity,
    rate_matrix,
    recent_tend,
    older_tend,
    destination,
    target_slot,
    live_counts,
    tile_ids,
    sensor,
    flame_flags,
):
    slot_count = fields.shape[0]
    peer_count = lax.axis_size(("mig", "pen"))
    myself = lax.axis_index(("mig", "pen"))
    slot_range = jnp.arange(slot_count, dtype=jnp.int32)
    peer_range = jnp.arange(peer_count, dtype=jnp.int32)
    keep_hot = (
        (destination[None, :] == myself) & (target_slot[None, :] == slot_range[:, None])
    ).astype(jnp.bfloat16)
    send_hot = (
        (destination[None, :] == peer_range[:, None]) & (peer_range[:, None] != myself)
    ).astype(jnp.bfloat16)
    slot_hot = (target_slot[:, None] == slot_range[None, :]).astype(jnp.bfloat16)
    outgoing_slots = jnp.dot(send_hot, slot_hot, preferred_element_type=jnp.float32).astype(
        jnp.bfloat16
    )
    outgoing_recent = jnp.einsum(
        "bi,isc->bsc", send_hot, recent_tend, preferred_element_type=jnp.float32
    ).astype(jnp.bfloat16)
    outgoing_older = jnp.einsum(
        "bi,isc->bsc", send_hot, older_tend, preferred_element_type=jnp.float32
    ).astype(jnp.bfloat16)
    arrived_recent, arrived_older, arrived_slots = side_by_side(
        (outgoing_recent, outgoing_older, outgoing_slots), ("mig", "pen"), 0, 0, 1
    )
    moved_recent = jnp.einsum(
        "ji,isc->jsc", keep_hot, recent_tend, preferred_element_type=jnp.float32
    ) + jnp.einsum("bj,bsc->jsc", arrived_slots, arrived_recent, preferred_element_type=jnp.float32)
    moved_older = jnp.einsum(
        "ji,isc->jsc", keep_hot, older_tend, preferred_element_type=jnp.float32
    ) + jnp.einsum("bj,bsc->jsc", arrived_slots, arrived_older, preferred_element_type=jnp.float32)
    expand = jnp.repeat(jnp.repeat(flame_flags.astype(jnp.float32), TE, axis=0), TE * TE, axis=1)
    raw_sensor = sensor * expand
    brick_rows = raw_sensor.shape[0]
    neighbour_planes = []
    for offset_by in (1, -1):
        neighbour_planes.append(
            passed_along(raw_sensor.astype(jnp.bfloat16), "pen", offset_by).astype(raw_sensor.dtype)
        )
    widened = jnp.concatenate([neighbour_planes[0], raw_sensor, neighbour_planes[1]], axis=0)
    filtered = jnp.dot(banded(brick_rows, brick_rows), widened, precision=lax.Precision.HIGHEST)
    local_thick = tile_thickening(filtered, TE, TZ, TCOL).reshape(slot_count)
    thick_table = whole_of(local_thick, GRP_MIG_PEN, (0, 2, 3, 1), 0)
    slot_thick = jnp.take(thick_table, tile_ids)
    tendencies = tendency(fields, ghosts, velocity, slot_thick, rate_matrix, TE)
    live_mask = (slot_range < live_counts[0]).astype(jnp.float32)[:, None, None]
    update = 23.0 / 12.0 * tendencies - 16.0 / 12.0 * moved_recent + 5.0 / 12.0 * moved_older
    new_fields = (fields + step_size * update) * live_mask
    new_tend = (tendencies * live_mask).astype(jnp.bfloat16)
    return (new_fields, new_tend, filtered)


def solution(mesh):
    finer = Mesh(
        mesh.devices.reshape(4, 2, mesh.shape["mig"], mesh.shape["pen"]),
        ("grp_0", "grp_1", "mig", "pen"),
    )
    placed = (
        P(GRP_MIG_PEN, None, None),
        P(GRP_MIG_PEN, None, None),
        P(None, GRP_MIG_PEN),
        P(),
        P(GRP_MIG_PEN, None, None),
        P(GRP_MIG_PEN, None, None),
        P(GRP_MIG_PEN),
        P(GRP_MIG_PEN),
        P(GRP_MIG_PEN),
        P(GRP_MIG_PEN),
        P("pen", GRP_MIG),
        P("pen", GRP_MIG),
    )
    return jax.shard_map(
        local,
        mesh=finer,
        in_specs=placed,
        out_specs=(P(GRP_MIG_PEN, None, None), P(GRP_MIG_PEN, None, None), P("pen", GRP_MIG)),
        check_vma=False,
    )
```

profile of v0, /device:TPU:1, one launch (start us, length us, event | category | flops | bytes accessed | tf_op | source)
XLA Modules:
  0.0 300.8 jit_solution(14106804295361804887)
XLA Ops:
  2.0 2.0 fusion.122
  3.9 2.5 collective-permute-start
  6.4 2.1 collective-permute-start.1
  8.5 2.2 fusion.15
  11.6 1.6 maximum_bitcast_fusion
  13.7 4.8 %reduce = bf16[16,73760]{1,0:T(8,128)(2,1)} reduce(bf16[16,1,73760]{2,0,1:T(8,128)(2,1)} %maximum_bitcast_fusion, bf16[]{:T(256)} %broadcast.576), dimensions={1}, to_apply=%copy.159.reduce_sub_computation | reduce | bytes 4720642 | tf_op jit(solution)/shard_map/all_to_all | solution.py:23
  18.5 3.8 %reshape.307 = bf16[16,2,36880]{2,1,0:T(2,128)(2,1)} reshape(bf16[16,73760]{1,0:T(8,128)(2,1)} %reduce) | data formatting | bytes 4720640
  22.3 5.7 %all-to-all-start = ((bf16[16,2,36880]{2,1,0:T(2,128)(2,1)}), bf16[16,2,36880]{2,1,0:T(2,128)(2,1)}, u32[]{:S(2)}, u32[]{:S(2)}) async-start(bf16[16,2,36880]{2,1,0:T(2,128)(2,1)} %reshape.307), calls=%async_computation | async-start | bytes 4734976 | tf_op jit(solution)/shard_map/all_to_all | solution.py:23
  33.3 2.9 fusion.89
  36.3 2.9 fusion.91
  39.2 5.3 %fusion.128 = (f32[32,9,4095]{2,0,1:T(8,128)}, f32[32,9,4095]{2,0,1:T(8,128)}) fusion(f32[32,9,4096]{2,0,1:T(8,128)S(1)} %bitcast.84), kind=kLoop, calls=%fused_computation.177 | loop fusion | bytes 18869760 | tf_op jit(solution)/shard_map/jit(_roll_static)/slice | solution.py:98
  44.5 5.3 %fusion.126 = (f32[32,9,4080]{2,0,1:T(8,128)}, f32[32,9,4080]{2,0,1:T(8,128)}) fusion(f32[32,9,4096]{2,0,1:T(8,128)S(1)} %bitcast.84), kind=kLoop, calls=%fused_computation.175 | loop fusion | bytes 18800640 | tf_op jit(solution)/shard_map/jit(_roll_static)/slice | solution.py:98
  49.8 4.3 %fusion.124 = (f32[32,9,3840]{2,0,1:T(8,128)}, f32[32,9,3840]{2,0,1:T(8,128)}) fusion(f32[32,9,4096]{2,0,1:T(8,128)S(1)} %bitcast.84), kind=kLoop, calls=%fused_computation.173 | loop fusion | bytes 17694720 | tf_op jit(solution)/shard_map/jit(_roll_static)/slice | solution.py:98
  58.5 0.9 fusion.130
  59.7 1.1 copy.142
  62.6 4.6 %convolution_bitcast_fusion.5 = f32[288,4096]{1,0:T(8,128)} fusion(f32[288,256]{1,0:T(8,128)S(1)} %reshape.268, s32[4096]{0:T(1024)S(1)} %copy-done.13, pred[4096]{0:T(1024)(128)(4,1)S(1)} %copy-done.29), kind=kOutput, calls=%fused_computation.31 | convolution fusion | flops 3625975808 | bytes 5033984 | tf_op jit(solution)/shard_map/dot_general | solution.py:94
  67.2 5.0 %convolution_bitcast_fusion.4 = f32[288,4096]{1,0:T(8,128)} fusion(f32[288,256]{1,0:T(8,128)S(1)} %reshape.270, s32[4096]{0:T(1024)S(1)} %copy-done.13, pred[4096]{0:T(1024)(128)(4,1)S(1)} %copy-done.28), kind=kOutput, calls=%fused_computation.30 | convolution fusion | flops 3625975808 | bytes 5033984 | tf_op jit(solution)/shard_map/dot_general | solution.py:94
  72.2 4.6 %convolution_bitcast_fusion.3 = f32[288,4096]{1,0:T(8,128)} fusion(f32[288,256]{1,0:T(8,128)S(1)} %reshape.272, s32[4096]{0:T(1024)S(1)} %copy-done.12, pred[4096]{0:T(1024)(128)(4,1)S(1)} %copy-done.27), kind=kOutput, calls=%fused_computation.29 | convolution fusion | flops 3625975808 | bytes 5033984 | tf_op jit(solution)/shard_map/dot_general | solution.py:94
  76.9 4.6 %convolution_bitcast_fusion.2 = f32[288,4096]{1,0:T(8,128)} fusion(f32[288,256]{1,0:T(8,128)S(1)} %reshape.274, s32[4096]{0:T(1024)S(1)} %copy-done.12, pred[4096]{0:T(1024)(128)(4,1)S(1)} %copy-done.26), kind=kOutput, calls=%fused_computation.28 | convolution fusion | flops 3625975808 | bytes 5033984 | tf_op jit(solution)/shard_map/dot_general | solution.py:94
  81.4 4.6 %convolution_bitcast_fusion.1 = f32[288,4096]{1,0:T(8,128)} fusion(f32[288,256]{1,0:T(8,128)S(1)} %reshape.276, s32[4096]{0:T(1024)S(1)} %fusion.79, pred[4096]{0:T(1024)(128)(4,1)S(1)} %copy-done.25), kind=kOutput, calls=%fused_computation.27 | convolution fusion | flops 3625975808 | bytes 5033984 | tf_op jit(solution)/shard_map/dot_general | solution.py:94
  86.1 4.6 %convolution_bitcast_fusion = f32[288,4096]{1,0:T(8,128)} fusion(f32[288,256]{1,0:T(8,128)S(1)} %reshape.278, s32[4096]{0:T(1024)S(1)} %fusion.79, pred[4096]{0:T(1024)(128)(4,1)S(1)} %copy-done.24), kind=kOutput, calls=%fused_computation.26 | convolution fusion | flops 3625975808 | bytes 5033984 | tf_op jit(solution)/shard_map/dot_general | solution.py:94
  90.7 2.4 broadcast_multiply_fusion
  93.1 6.3 %reshape.269 = f32[32,9,4096]{2,1,0:T(8,128)} reshape(f32[288,4096]{1,0:T(8,128)} %convolution_bitcast_fusion.5) | data formatting | bytes 9437184 | tf_op jit(solution)/shard_map/reshape | solution.py:95
  99.4 6.2 %reshape.271 = f32[32,9,4096]{2,1,0:T(8,128)} reshape(f32[288,4096]{1,0:T(8,128)} %convolution_bitcast_fusion.4) | data formatting | bytes 9437184 | tf_op jit(solution)/shard_map/reshape | solution.py:95
  105.5 6.3 %reshape.273 = f32[32,9,4096]{2,1,0:T(8,128)} reshape(f32[288,4096]{1,0:T(8,128)} %convolution_bitcast_fusion.3) | data formatting | bytes 9437184 | tf_op jit(solution)/shard_map/reshape | solution.py:95
  111.8 6.2 %reshape.275 = f32[32,9,4096]{2,1,0:T(8,128)} reshape(f32[288,4096]{1,0:T(8,128)} %convolution_bitcast_fusion.2) | data formatting | bytes 9437184 | tf_op jit(solution)/shard_map/reshape | solution.py:95
  118.0 6.2 %reshape.277 = f32[32,9,4096]{2,1,0:T(8,128)} reshape(f32[288,4096]{1,0:T(8,128)} %convolution_bitcast_fusion.1) | data formatting | bytes 9437184 | tf_op jit(solution)/shard_map/reshape | solution.py:95
  124.2 6.4 %reshape.279 = f32[32,9,4096]{2,1,0:T(8,128)} reshape(f32[288,4096]{1,0:T(8,128)} %convolution_bitcast_fusion) | data formatting | bytes 9437184 | tf_op jit(solution)/shard_map/reshape | solution.py:95
  130.6 8.8 %copy.212 = f32[32,9,4095]{2,1,0:T(8,128)} copy(f32[32,9,4095]{2,0,1:T(8,128)} %get-tuple-element.35) | data formatting | bytes 9434880
  139.4 6.3 %copy.213 = f32[32,9,4095]{2,1,0:T(8,128)} copy(f32[32,9,4095]{2,0,1:T(8,128)S(1)} %bitcast.92) | data formatting | bytes 9434880
  145.7 6.2 %copy.216 = f32[32,9,4080]{2,1,0:T(8,128)} copy(f32[32,9,4080]{2,0,1:T(8,128)S(1)} %bitcast.90) | data formatting | bytes 9400320
  152.0 6.5 %copy.217 = f32[32,9,4080]{2,1,0:T(8,128)} copy(f32[32,9,4080]{2,0,1:T(8,128)S(1)} %bitcast.88) | data formatting | bytes 9400320
  158.5 5.9 %copy.220 = f32[32,9,3840]{2,1,0:T(8,128)} copy(f32[32,9,3840]{2,0,1:T(8,128)S(1)} %bitcast.96) | data formatting | bytes 8847360
  164.4 5.9 %copy.221 = f32[32,9,3840]{2,1,0:T(8,128)} copy(f32[32,9,3840]{2,0,1:T(8,128)S(1)} %bitcast.94) | data formatting | bytes 8847360
  174.6 1.0 convert_element_type.93
  175.6 1.0 convert_element_type.94
  176.6 2.3 broadcast_minimum_fusion
  179.3 8.0 %all-gather.3 = f32[4,1,32]{2,1,0:T(1,128)S(1)} all-gather(f32[1,1,32]{2,1,0:T(1,128)S(1)} %reshape.296), channel_id=1, replica_groups=mesh['grp_0'=4,'grp_1'=2,'mig'=4,'pen'=4] {'grp_0'}, dimensions={0}, use_global_device_ids=true | all-gather | bytes 640 | tf_op jit(solution)/shard_map/all_gather | solution.py:48
  187.2 8.6 %all-gather.4 = f32[4,4,32]{2,1,0:T(4,128)S(1)} all-gather(f32[1,4,32]{2,1,0:T(4,128)S(1)} %bitcast.111), channel_id=2, replica_groups=mesh['grp_0'=4,'grp_1'=2,'mig'=4,'pen'=4] {'mig'}, dimensions={0}, use_global_device_ids=true | all-gather | bytes 2560 | tf_op jit(solution)/shard_map/all_gather | solution.py:48
  195.8 9.3 %all-gather.1 = f32[16,4,32]{2,1,0:T(4,128)S(1)} all-gather(f32[4,4,32]{2,1,0:T(4,128)S(1)} %all-gather.4), channel_id=3, replica_groups=mesh['grp_0'=4,'grp_1'=2,'mig'=4,'pen'=4] {'pen'}, dimensions={0}, use_global_device_ids=true | all-gather | bytes 10240 | tf_op jit(solution)/shard_map/all_gather | solution.py:48
  205.1 10.9 %all-gather.2 = f32[8,4,4,32]{3,2,1,0:T(4,128)S(1)} all-gather(f32[4,4,4,32]{3,2,1,0:T(4,128)S(1)} %bitcast.109), channel_id=4, replica_groups=mesh['grp_0'=4,'grp_1'=2,'mig'=4,'pen'=4] {'grp_1'}, dimensions={0}, use_global_device_ids=true | all-gather | bytes 24576 | tf_op jit(solution)/shard_map/all_gather | solution.py:48
  216.8 13.7 %reshape.308 = bf16[16,1,73760]{2,1,0:T(2,128)(2,1)} reshape(bf16[16,2,36880]{2,1,0:T(2,128)(2,1)} %all-to-all-done) | data formatting | bytes 4720640
  230.5 2.6 copy.225
  233.4 2.9 fusion.52
  236.3 3.0 fusion.49
  239.4 49.6 %multiply_convert_fusion = (bf16[32,9,4096]{2,1,0:T(8,128)(2,1)}, f32[32,9,4096]{2,1,0:T(8,128)}) fusion(f32[32]{0:T(128)S(1)} %compare_convert_fusion.2, f32[32,9,4096]{2,0,1:T(8,128)} %fusion.49, f32[32,9,4096]{2,0,1:T(8,128)} %fusion.89, f32[32,9,4096]{2,0,1:T(8,128)} %fusion.52, f32[32,9,4096]{2,0,1:T(8,128)} %fusion.91, f32[32,9,4096]{2,0,1:T(8,128)} %param.12, ...), kind=kOutput, calls=%fused_computation.25 | convolution fusion | flops 186384384 | bytes 92111936 | tf_op jit(solution)/shard_map/sk,nkc->nsc/dot_general | solution.py:113
  289.0 8.5 %copy.167 = f32[32,9,4096]{2,0,1:T(8,128)} copy(f32[32,9,4096]{2,1,0:T(8,128)} %get-tuple-element.23) | data formatting | bytes 9437184
  297.4 2.8 copy.168
  (170 shorter events, 19.3 us)
Async XLA Ops:
  0.6 10.2 %copy-start = (bf16[32,9,4096]{2,0,1:T(8,128)(2,1)S(1)}, bf16[32,9,4096]{2,0,1:T(8,128)(2,1)}, u32[]{:S(2)}) copy-start(bf16[32,9,4096]{2,0,1:T(8,128)(2,1)} %param.17) | copy-start | bytes 7077892
  0.6 10.2 %copy-start.31 = (s32[32]{0:T(128)S(1)}, s32[32]{0:T(128)}, u32[]{:S(2)}) copy-start(s32[32]{0:T(128)} %param.18) | copy-start | bytes 388
  3.9 170.6 %collective-permute-start = (bf16[32,4096]{1,0:T(8,128)(2,1)}, bf16[32,4096]{1,0:T(8,128)(2,1)}, u32[]{:S(2)}, u32[]{:S(2)}) collective-permute-start(bf16[32,4096]{1,0:T(8,128)(2,1)} %get-tuple-element.20), channel_id=1, source_target_pairs={{0,1},{1,2},{2,3},{3,0},{4,5},{5,6},{6,7},{7,4},{8,9},{9,10},{10,1... | collective-permute-start | bytes 786440 | tf_op jit(solution)/shard_map/ppermute | solution.py:36
  6.4 169.2 %collective-permute-start.1 = (bf16[32,4096]{1,0:T(8,128)(2,1)}, bf16[32,4096]{1,0:T(8,128)(2,1)}, u32[]{:S(2)}, u32[]{:S(2)}) collective-permute-start(bf16[32,4096]{1,0:T(8,128)(2,1)} %get-tuple-element.20), channel_id=1, source_target_pairs={{0,3},{1,0},{2,1},{3,2},{4,7},{5,4},{6,5},{7,6},{8,11},{9,8},{10,9... | collective-permute-start | bytes 786440 | tf_op jit(solution)/shard_map/ppermute | solution.py:36
  22.3 16.9 %slice-start = ((s8[4718592]{0:T(1024)(128)(4,1)}), s8[524288]{0:T(1024)(128)(4,1)S(1)}, s32[]{:S(2)}) async-start(s8[4718592]{0:T(1024)(128)(4,1)} %bitcast.83), calls=%async_computation.1 | async-start | bytes 1048576
  22.3 194.5 %all-to-all-start = ((bf16[16,2,36880]{2,1,0:T(2,128)(2,1)}), bf16[16,2,36880]{2,1,0:T(2,128)(2,1)}, u32[]{:S(2)}, u32[]{:S(2)}) async-start(bf16[16,2,36880]{2,1,0:T(2,128)(2,1)} %reshape.307), calls=%async_computation | async-start | bytes 4734976 | tf_op jit(solution)/shard_map/all_to_all | solution.py:23
  28.0 8.3 %copy-start.3 = (bf16[32,9,4096]{2,0,1:T(8,128)(2,1)S(1)}, bf16[32,9,4096]{2,0,1:T(8,128)(2,1)}, u32[]{:S(2)}) copy-start(bf16[32,9,4096]{2,0,1:T(8,128)(2,1)} %param.16) | copy-start | bytes 7077892
  33.3 5.9 %slice-start.1 = ((s8[4718592]{0:T(1024)(128)(4,1)}), s8[4194304]{0:T(1024)(128)(4,1)S(1)}, s32[]{:S(2)}) async-start(s8[4718592]{0:T(1024)(128)(4,1)} %bitcast.83), calls=%async_computation.2 | async-start | bytes 8388608
  49.8 8.7 %copy-start.35 = (s32[32]{0:T(128)S(1)}, s32[32]{0:T(128)}, u32[]{:S(2)}) copy-start(s32[32]{0:T(128)} %param.21) | copy-start | bytes 388
  54.1 4.4 %copy-start.5 = (f32[32,9,1536]{2,0,1:T(8,128)S(1)}, f32[32,9,1536]{2,0,1:T(8,128)}, u32[]{:S(2)}) copy-start(f32[32,9,1536]{2,0,1:T(8,128)} %param.13) | copy-start | bytes 5308420
  59.4 3.1 %copy-start.13 = (s32[4096]{0:T(1024)S(1)}, s32[4096]{0:T(1024)}, u32[]{:S(2)}) copy-start(s32[4096]{0:T(1024)} %fusion.62) | copy-start | bytes 49156
  59.4 3.1 %copy-start.29 = (pred[4096]{0:T(1024)(128)(4,1)S(1)}, pred[4096]{0:T(1024)(128)(4,1)}, u32[]{:S(2)}) copy-start(pred[4096]{0:T(1024)(128)(4,1)} %fusion.77) | copy-start | bytes 12292
  61.9 5.4 %copy-start.28 = (pred[4096]{0:T(1024)(128)(4,1)S(1)}, pred[4096]{0:T(1024)(128)(4,1)}, u32[]{:S(2)}) copy-start(pred[4096]{0:T(1024)(128)(4,1)} %fusion.75) | copy-start | bytes 12292
  67.2 5.0 %copy-start.12 = (s32[4096]{0:T(1024)S(1)}, s32[4096]{0:T(1024)}, u32[]{:S(2)}) copy-start(s32[4096]{0:T(1024)} %fusion.61) | copy-start | bytes 49156
  67.2 5.0 %copy-start.27 = (pred[4096]{0:T(1024)(128)(4,1)S(1)}, pred[4096]{0:T(1024)(128)(4,1)}, u32[]{:S(2)}) copy-start(pred[4096]{0:T(1024)(128)(4,1)} %broadcast_compare_fusion.1) | copy-start | bytes 12292
  72.2 4.6 %copy-start.26 = (pred[4096]{0:T(1024)(128)(4,1)S(1)}, pred[4096]{0:T(1024)(128)(4,1)}, u32[]{:S(2)}) copy-start(pred[4096]{0:T(1024)(128)(4,1)} %broadcast_compare_fusion) | copy-start | bytes 12292
  76.8 4.6 %copy-start.25 = (pred[4096]{0:T(1024)(128)(4,1)S(1)}, pred[4096]{0:T(1024)(128)(4,1)}, u32[]{:S(2)}) copy-start(pred[4096]{0:T(1024)(128)(4,1)} %fusion.59) | copy-start | bytes 12292
  81.4 4.6 %copy-start.24 = (pred[4096]{0:T(1024)(128)(4,1)S(1)}, pred[4096]{0:T(1024)(128)(4,1)}, u32[]{:S(2)}) copy-start(pred[4096]{0:T(1024)(128)(4,1)} %fusion.57) | copy-start | bytes 12292
  81.4 9.2 %slice-start.2 = ((s8[4718592]{0:T(1024)(128)(4,1)}), s8[4194304]{0:T(1024)(128)(4,1)S(1)}, s32[]{:S(2)}) async-start(s8[4718592]{0:T(1024)(128)(4,1)} %bitcast.85), calls=%async_computation.3 | async-start | bytes 8388608
  86.0 4.6 %slice-start.3 = ((s8[4718592]{0:T(1024)(128)(4,1)}), s8[524288]{0:T(1024)(128)(4,1)S(1)}, s32[]{:S(2)}) async-start(s8[4718592]{0:T(1024)(128)(4,1)} %bitcast.85), calls=%async_computation.4 | async-start | bytes 1048576
  124.2 15.2 %slice-start.8 = ((s8[4718592]{0:T(1024)(128)(4,1)}), s8[524288]{0:T(1024)(128)(4,1)S(1)}, s32[]{:S(2)}) async-start(s8[4718592]{0:T(1024)(128)(4,1)} %bitcast.91), calls=%async_computation.9 | async-start | bytes 1048576
  130.6 8.8 %slice-start.9 = ((s8[4718592]{0:T(1024)(128)(4,1)}), s8[4194304]{0:T(1024)(128)(4,1)S(1)}, s32[]{:S(2)}) async-start(s8[4718592]{0:T(1024)(128)(4,1)} %bitcast.91), calls=%async_computation.10 | async-start | bytes 8388608
  130.6 15.1 %slice-start.6 = ((s8[4718592]{0:T(1024)(128)(4,1)}), s8[4194304]{0:T(1024)(128)(4,1)S(1)}, s32[]{:S(2)}) async-start(s8[4718592]{0:T(1024)(128)(4,1)} %bitcast.89), calls=%async_computation.7 | async-start | bytes 8388608
  139.4 6.3 %slice-start.7 = ((s8[4718592]{0:T(1024)(128)(4,1)}), s8[524288]{0:T(1024)(128)(4,1)S(1)}, s32[]{:S(2)}) async-start(s8[4718592]{0:T(1024)(128)(4,1)} %bitcast.89), calls=%async_computation.8 | async-start | bytes 1048576
  139.4 12.5 %slice-start.4 = ((s8[4718592]{0:T(1024)(128)(4,1)}), s8[4194304]{0:T(1024)(128)(4,1)S(1)}, s32[]{:S(2)}) async-start(s8[4718592]{0:T(1024)(128)(4,1)} %bitcast.87), calls=%async_computation.5 | async-start | bytes 8388608
  145.7 6.2 %slice-start.5 = ((s8[4718592]{0:T(1024)(128)(4,1)}), s8[524288]{0:T(1024)(128)(4,1)S(1)}, s32[]{:S(2)}) async-start(s8[4718592]{0:T(1024)(128)(4,1)} %bitcast.87), calls=%async_computation.6 | async-start | bytes 1048576
  145.7 12.8 %slice-start.12 = ((s8[4423680]{0:T(1024)(128)(4,1)}), s8[4194304]{0:T(1024)(128)(4,1)S(1)}, s32[]{:S(2)}) async-start(s8[4423680]{0:T(1024)(128)(4,1)} %bitcast.95), calls=%async_computation.13 | async-start | bytes 8388608
  145.7 18.7 %slice-start.10 = ((s8[4423680]{0:T(1024)(128)(4,1)}), s8[229376]{0:T(1024)(128)(4,1)S(1)}, s32[]{:S(2)}) async-start(s8[4423680]{0:T(1024)(128)(4,1)} %bitcast.93), calls=%async_computation.11 | async-start | bytes 458752
  151.9 6.5 %slice-start.13 = ((s8[4423680]{0:T(1024)(128)(4,1)}), s8[229376]{0:T(1024)(128)(4,1)S(1)}, s32[]{:S(2)}) async-start(s8[4423680]{0:T(1024)(128)(4,1)} %bitcast.95), calls=%async_computation.14 | async-start | bytes 458752
  151.9 12.4 %slice-start.11 = ((s8[4423680]{0:T(1024)(128)(4,1)}), s8[4194304]{0:T(1024)(128)(4,1)S(1)}, s32[]{:S(2)}) async-start(s8[4423680]{0:T(1024)(128)(4,1)} %bitcast.93), calls=%async_computation.12 | async-start | bytes 8388608
  164.4 6.0 %copy-start.7 = (f32[32,9,256]{2,0,1:T(8,128)S(1)}, f32[32,9,256]{2,0,1:T(8,128)}, u32[]{:S(2)}) copy-start(f32[32,9,256]{2,0,1:T(8,128)} %get-tuple-element.25) | copy-start | bytes 884740
  164.4 6.2 %copy-start.6 = (f32[32,9,256]{2,0,1:T(8,128)S(1)}, f32[32,9,256]{2,0,1:T(8,128)}, u32[]{:S(2)}) copy-start(f32[32,9,256]{2,0,1:T(8,128)} %get-tuple-element.24) | copy-start | bytes 884740
  164.4 6.3 %copy-start.17 = (f32[32,9,1]{2,0,1:T(8,128)S(1)}, f32[32,9,1]{2,0,1:T(8,128)}, u32[]{:S(2)}) copy-start(f32[32,9,1]{2,0,1:T(8,128)} %get-tuple-element.33) | copy-start | bytes 3460
  164.4 7.1 %copy-start.16 = (f32[32,9,1]{2,0,1:T(8,128)S(1)}, f32[32,9,1]{2,0,1:T(8,128)}, u32[]{:S(2)}) copy-start(f32[32,9,1]{2,0,1:T(8,128)} %get-tuple-element.32) | copy-start | bytes 3460
  164.4 7.9 %copy-start.15 = (f32[32,9,16]{2,0,1:T(8,128)S(1)}, f32[32,9,16]{2,0,1:T(8,128)}, u32[]{:S(2)}) copy-start(f32[32,9,16]{2,0,1:T(8,128)} %get-tuple-element.29) | copy-start | bytes 55300
  164.4 8.7 %copy-start.14 = (f32[32,9,16]{2,0,1:T(8,128)S(1)}, f32[32,9,16]{2,0,1:T(8,128)}, u32[]{:S(2)}) copy-start(f32[32,9,16]{2,0,1:T(8,128)} %get-tuple-element.28) | copy-start | bytes 55300
  164.4 10.1 %copy-start.33 = (f32[3,32]{1,0:T(4,128)S(1)}, f32[3,32]{1,0:T(4,128)}, u32[]{:S(2)}) copy-start(f32[3,32]{1,0:T(4,128)} %param.14) | copy-start | bytes 1156
  170.3 6.2 %copy-start.4 = (f32[32,4096]{1,0:T(8,128)S(1)}, f32[32,4096]{1,0:T(8,128)}, u32[]{:S(2)}) copy-start(f32[32,4096]{1,0:T(8,128)} %get-tuple-element.21) | copy-start | bytes 1572868
  170.3 6.2 %copy-start.34 = (s32[96]{0:T(128)S(1)}, s32[96]{0:T(128)}, u32[]{:S(2)}) copy-start(s32[96]{0:T(128)} %iota_add_fusion) | copy-start | bytes 1156
  233.3 6.0 %copy-start.18 = (f32[4096]{0:T(1024)S(1)}, f32[4096]{0:T(1024)}, u32[]{:S(2)}) copy-start(f32[4096]{0:T(1024)} %get-tuple-element.49) | copy-start | bytes 49156
  233.3 6.0 %copy-start.19 = (f32[4096]{0:T(1024)S(1)}, f32[4096]{0:T(1024)}, u32[]{:S(2)}) copy-start(f32[4096]{0:T(1024)} %get-tuple-element.50) | copy-start | bytes 49156
  233.3 6.0 %copy-start.20 = (f32[4096]{0:T(1024)S(1)}, f32[4096]{0:T(1024)}, u32[]{:S(2)}) copy-start(f32[4096]{0:T(1024)} %get-tuple-element.51) | copy-start | bytes 49156
  233.3 6.0 %copy-start.21 = (f32[4096]{0:T(1024)S(1)}, f32[4096]{0:T(1024)}, u32[]{:S(2)}) copy-start(f32[4096]{0:T(1024)} %get-tuple-element.52) | copy-start | bytes 49156
  233.4 6.0 %copy-start.22 = (f32[4096]{0:T(1024)S(1)}, f32[4096]{0:T(1024)}, u32[]{:S(2)}) copy-start(f32[4096]{0:T(1024)} %get-tuple-element.53) | copy-start | bytes 49156
  233.4 6.0 %copy-start.23 = (f32[4096]{0:T(1024)S(1)}, f32[4096]{0:T(1024)}, u32[]{:S(2)}) copy-start(f32[4096]{0:T(1024)} %get-tuple-element.54) | copy-start | bytes 49156
  233.4 6.0 %copy-start.30 = (f32[9,9]{1,0:T(8,128)S(1)}, f32[9,9]{1,0:T(8,128)}, u32[]{:S(2)}) copy-start(f32[9,9]{1,0:T(8,128)} %param.15) | copy-start | bytes 976
  288.9 8.5 %copy-start.2 = (bf16[32,9,4096]{2,1,0:T(8,128)(2,1)S(1)}, bf16[32,9,4096]{2,1,0:T(8,128)(2,1)}, u32[]{:S(2)}) copy-start(bf16[32,9,4096]{2,1,0:T(8,128)(2,1)} %get-tuple-element.22) | copy-start | bytes 7077892
  289.0 11.3 %copy-start.1 = (bf16[32,9,4096]{2,0,1:T(8,128)(2,1)S(1)}, bf16[32,9,4096]{2,0,1:T(8,128)(2,1)}, u32[]{:S(2)}) copy-start(bf16[32,9,4096]{2,0,1:T(8,128)(2,1)} %param.17) | copy-start | bytes 7077892
  (5 other events, 12.9 us)
where the time goes:
time: 306 us; the launch traced here: 301 us
  local copies, waits for them, and re-layouts  135 us (44%)
  matrix products  94.5 us (31%)
  blocking collectives  36.7 us (12%)
  other arithmetic  21.5 us (7%)
  starting transfers between devices  10.3 us (3%)
    unnamed x120, local copies, waits for them, and re-layouts  75.3 us
    dot_general x1, matrix products, tendency(): jnp.einsum('sk,nkc->nsc', rate_matrix, fields * burning[:, None, :], prec...  49.6 us
    reshape x6, local copies, waits for them, and re-layouts, outside(): return placed.reshape(lead, species, tile_cells)  37.5 us
    all_gather x4, blocking collectives, all_blocks(): blocks = lax.all_gather(blocks, axes[k])  36.7 us
    dot_general x6, matrix products, outside(): jnp.dot(face_values, placement(tile_edge, which), precision=lax.Precision...  28 us
    slice x6, local copies, waits for them, and re-layouts, inside(): return jnp.roll(fields, shift, axis=2) * interior.astype(jnp.float32)  17.4 us
    all_to_all x2, other arithmetic, side_by_side(): lax.all_to_all(both, axis, split_axis=split_dim, concat_axis=concat_dim,...  6.32 us
  transfers between devices with their start and end apart: 3, of which 0 were waited for; matrix products, arithmetic and copies ran while one was open for 55% of the time, Pallas kernels for 0%

commit v1 on v0

v1 whole, which is shorter than its diff:
```python
import functools
import math

import jax
import jax.numpy as jnp
from jax import lax
from jax.experimental import pallas as pl
from jax.experimental.pallas import tpu as pltpu
from jax.sharding import PartitionSpec as P

S = 9
SLOTS = 32
CELLS = 4096
HALF = CELLS // 2
FACE = 256
PLANES = 16
BZ = 32
COLS = 4096
ALL_AXES = ("grp", "mig", "pen")
MESH = pl.DeviceIdType.MESH
N_GRP, N_MIG, N_PEN = 8, 4, 4
PEERS = N_MIG * N_PEN

VISCOUS = 0.05
STEP = 0.25
SIGMA = BZ / 2.0
GAUSS_TOTAL = sum(math.exp(-k * k / (2.0 * SIGMA * SIGMA)) for k in range(-BZ, BZ + 1))
CHUNKS = ((0, 3), (3, 6), (6, 9))


def split(x):
    hi = x.astype(jnp.bfloat16)
    return hi, (x - hi.astype(jnp.float32)).astype(jnp.bfloat16)


def iota(shape, dim):
    return lax.broadcasted_iota(jnp.int32, shape, dim)


def column(row):
    same = iota((SLOTS, SLOTS), 0) == iota((SLOTS, SLOTS), 1)
    spread = jnp.broadcast_to(row, (SLOTS, SLOTS))
    return jnp.sum(jnp.where(same, spread, jnp.zeros_like(spread)), axis=1, keepdims=True)


def kernel(
    fields,
    ghosts,
    velocity,
    rate,
    recent,
    older,
    destination,
    target,
    live,
    ids,
    sensor,
    flags,
    new_fields,
    new_tend,
    filtered,
    padded,
    faces,
    rec,
    old,
    out_msg,
    in_msg,
    out_slot,
    in_slot,
    lap,
    adv,
    react,
    sens,
    raw_hi,
    raw_lo,
    prev,
    nxt,
    table,
    vcol,
    local_sem,
    halo_send,
    halo_recv,
    slot_send,
    slot_recv,
    msg_send,
    msg_recv,
    grp_send,
    grp_recv,
    blk_send,
    blk_recv,
):
    g, m, p = (lax.axis_index(a) for a in ALL_AXES)
    group_at = m * N_PEN + p

    def peer(k):
        return (g, lax.rem(m + k // N_PEN, N_MIG), lax.rem(p + k % N_PEN, N_PEN))

    def grp_peer(k):
        return (lax.rem(g + k, N_GRP), m, p)

    in_msg[:, 0:16, :] = jnp.zeros((S, 16, HALF), jnp.bfloat16)
    in_slot[0:8, :] = jnp.full((8, 128), -1.0, jnp.float32)

    barrier = pltpu.get_barrier_semaphore()
    for k in range(1, PEERS):
        pl.semaphore_signal(barrier, inc=1, device_id=peer(k), device_id_type=MESH)
    for k in range(1, N_GRP):
        pl.semaphore_signal(barrier, inc=1, device_id=grp_peer(k), device_id_type=MESH)

    loads = [
        pltpu.make_async_copy(sensor, sens, local_sem.at[0]),
        pltpu.make_async_copy(recent, rec, local_sem.at[1]),
        pltpu.make_async_copy(older, old, local_sem.at[2]),
        pltpu.make_async_copy(fields, padded.at[:, :, FACE : FACE + CELLS], local_sem.at[3]),
        pltpu.make_async_copy(ghosts.at[:, :, 0:FACE], padded.at[:, :, 0:FACE], local_sem.at[4]),
        pltpu.make_async_copy(
            ghosts.at[:, :, FACE : 2 * FACE],
            padded.at[:, :, FACE + CELLS : 2 * FACE + CELLS],
            local_sem.at[5],
        ),
        pltpu.make_async_copy(ghosts.at[:, :, 2 * FACE : 6 * FACE], faces, local_sem.at[6]),
    ]
    for copy in loads:
        copy.start()

    dest = destination[...]
    slot = target[...]
    row_k = iota((2 * PEERS, 4 * SLOTS), 0)
    col_c = iota((2 * PEERS, 4 * SLOTS), 1)
    dest4 = jnp.concatenate([dest] * 4, axis=1)
    k_of = row_k >> 1
    peer_of = ((m + (k_of >> 2)) & 3) * 4 + ((p + (k_of & 3)) & 3)
    hot = (jnp.broadcast_to(dest4, row_k.shape) == peer_of) & (k_of > 0)
    weight = jnp.where((col_c >> 5) & 1 == 0, -16.0, 5.0)
    same_half = (col_c >> 6) == (row_k & 1)
    select = jnp.where(hot & same_half, weight, 0.0).astype(jnp.bfloat16)

    hot32 = hot[:, 0:SLOTS]
    slot_rows = jnp.broadcast_to(slot.astype(jnp.float32), hot32.shape)
    found = jnp.sum(jnp.where(hot32, slot_rows + 1.0, 0.0), axis=1, keepdims=True) - 1.0
    out_slot[...] = jnp.broadcast_to(found, (2 * PEERS, 128))

    live_col = iota((SLOTS, 1), 0) < live[0]
    mask = jnp.where(live_col, 1.0, 0.0)
    keep_row = iota((SLOTS, 2 * SLOTS), 0)
    keep_col = iota((SLOTS, 2 * SLOTS), 1)
    dest2 = jnp.broadcast_to(jnp.concatenate([dest] * 2, axis=1), keep_row.shape)
    slot2 = jnp.broadcast_to(jnp.concatenate([slot] * 2, axis=1), keep_row.shape)
    kept = (dest2 == group_at) & (slot2 == keep_row)
    keep = jnp.where(kept, jnp.where(keep_col < SLOTS, -16.0, 5.0), 0.0).astype(jnp.bfloat16)

    for d in range(3):
        vcol[d] = jnp.broadcast_to(-0.5 * column(velocity[d : d + 1, :]), (SLOTS, 128))

    loads[0].wait()
    for t in range(2):
        for j in range(16):
            flag = flags[t, j].astype(jnp.float32)
            at = (slice(t * 16, t * 16 + 16), slice(j * 256, j * 256 + 256))
            hi, lo = split(sens[at] * flag)
            raw_hi[at] = hi
            raw_lo[at] = lo

    loads[1].wait()
    loads[2].wait()

    @pl.loop(0, S)
    def _(s):
        for c in range(4):
            low = slice(c * 512, c * 512 + 512)
            high = slice(HALF + c * 512, HALF + c * 512 + 512)
            both = jnp.concatenate([rec[s, :, low], old[s, :, low], rec[s, :, high], old[s, :, high]], axis=0)
            out_msg[s, :, low] = jnp.dot(select, both, preferred_element_type=jnp.float32).astype(jnp.bfloat16)

    pl.semaphore_wait(barrier, PEERS - 1 + N_GRP - 1)

    halos = [
        pltpu.make_async_remote_copy(
            raw_hi, prev, halo_send.at[0], halo_recv.at[0], device_id=peer(1), device_id_type=MESH
        ),
        pltpu.make_async_remote_copy(
            raw_hi, nxt, halo_send.at[1], halo_recv.at[1], device_id=peer(3), device_id_type=MESH
        ),
    ]
    for copy in halos:
        copy.start()
    slots = []
    for k in range(1, PEERS):
        rows = slice(2 * k, 2 * k + 2)
        slots.append(
            pltpu.make_async_remote_copy(
                out_slot.at[rows, :], in_slot.at[rows, :], slot_send.at[k], slot_recv.at[k], device_id=peer(k), device_id_type=MESH
            )
        )
    for copy in slots:
        copy.start()
    moves = []
    for c, (s0, s1) in enumerate(CHUNKS):
        for k in range(1, PEERS):
            at = (slice(s0, s1), slice(2 * k, 2 * k + 2), slice(None))
            moves.append(
                pltpu.make_async_remote_copy(
                    out_msg.at[at], in_msg.at[at], msg_send.at[c, k], msg_recv.at[c, k], device_id=peer(k), device_id_type=MESH
                )
            )
    per_chunk = PEERS - 1
    for copy in moves[: 2 * per_chunk]:
        copy.start()

    for copy in loads[3:]:
        copy.wait()
    lane = iota((8, 128), 1)
    lane_z = lane & 15
    first_z = lane_z == 0
    last_z = lane_z == 15
    first_y = lane < 16
    last_y = lane >= 112

    def stencil(step):
        rows = pl.ds(pl.multiple_of((step // PLANES) * 8, 8), 8)
        x = step % PLANES
        at_face = (x // 8) * 128
        in_face = (x % 8) * 16
        idx_y = in_face + lane_z
        idx_z = [in_face + t * 8 + (lane >> 4) for t in range(2)]
        vx, vy, vz = (vcol[d, rows, :] for d in range(3))

        def face(s, which):
            return faces[s, rows, pl.ds(pl.multiple_of(which * FACE + at_face, 128), 128)]

        def plane(s, by, t):
            return padded[s, rows, pl.ds(pl.multiple_of((x + by) * FACE + t * 128, 128), 128)]

        def put(ref, s, t, value):
            ref[s, rows, pl.ds(pl.multiple_of(x * FACE + t * 128, 128), 128)] = value

        def pick(source, idx):
            return jnp.take_along_axis(source, idx, axis=1)

        for s in range(S):
            now = [plane(s, 1, t) for t in range(2)]
            down = [pltpu.roll(v, 16, 1) for v in now]
            up = [pltpu.roll(v, 112, 1) for v in now]
            y_low = [
                jnp.where(first_y, pick(face(s, 0), idx_y), down[0]),
                jnp.where(first_y, down[0], down[1]),
            ]
            y_high = [
                jnp.where(last_y, up[1], up[0]),
                jnp.where(last_y, pick(face(s, 1), idx_y), up[1]),
            ]
            for t in range(2):
                z_low = jnp.where(first_z, pick(face(s, 2), idx_z[t]), pltpu.roll(now[t], 1, 1))
                z_high = jnp.where(last_z, pick(face(s, 3), idx_z[t]), pltpu.roll(now[t], 127, 1))
                x_low = plane(s, 0, t)
                x_high = plane(s, 2, t)
                total = ((x_low + x_high) + (y_low[t] + y_high[t])) + (z_low + z_high)
                put(lap, s, t, VISCOUS * (total - 6.0 * now[t]))
                put(adv, s, t, vx * (x_high - x_low) + vy * (y_high[t] - y_low[t]) + vz * (z_high - z_low))
        for t in range(2):
            f = [plane(s, 1, t) for s in range(S)]
            burning = f[0] * f[1]
            f = [v * burning for v in f]
            for s in range(S):
                total = rate[s, 0] * f[0]
                for k in range(1, S):
                    total = total + rate[s, k] * f[k]
                put(react, s, t, total)

    pl.loop(0, 32)(stencil)

    for copy in halos:
        copy.wait_recv()
    r = iota((BZ, BZ), 0)
    q = iota((BZ, BZ), 1)

    def gauss(offset):
        off = jnp.abs(offset)
        d = off.astype(jnp.float32)
        w = jnp.where(off <= BZ, jnp.exp(-d * d / (2.0 * SIGMA * SIGMA)), 0.0)
        return split(w / GAUSS_TOTAL)

    own_hi, own_lo = gauss(r - q)
    prev_hi, prev_lo = gauss(r + BZ - q)
    next_hi, next_lo = gauss(q + BZ - r)
    bands = jnp.concatenate([own_hi, own_lo, own_hi, prev_hi, prev_lo, next_hi, next_lo], axis=1)
    wide = iota((1, 128), 1)
    sums = jnp.zeros((1, 128), jnp.float32)
    for j in range(16):
        cols = slice(j * 256, j * 256 + 256)
        own, back, ahead = raw_hi[:, cols], prev[:, cols], nxt[:, cols]
        planes = jnp.concatenate([own, own, raw_lo[:, cols], back, back, ahead, ahead], axis=0)
        value = jnp.dot(bands, planes, preferred_element_type=jnp.float32)
        filtered[:, cols] = value
        clipped = jnp.minimum(value, 1.0)
        for t in range(2):
            part = jnp.sum(clipped[t * 16 : t * 16 + 16, :], axis=0, keepdims=True)
            part = jnp.sum(part, axis=1, keepdims=True)
            sums = sums + jnp.where(wide == t * 16 + j, part, 0.0)
    mine = group_at * N_GRP + g
    table[pl.ds(mine, 1), :] = 1.0 + 4.0 * (sums * (1.0 / 4096.0))

    rows_sent = []
    for k in range(1, N_GRP):
        row = table.at[pl.ds(mine, 1), :]
        rows_sent.append(
            pltpu.make_async_remote_copy(row, row, grp_send.at[k], grp_recv.at[k], device_id=grp_peer(k), device_id_type=MESH)
        )
    for copy in rows_sent:
        copy.start()

    pl.loop(32, 48)(stencil)

    for copy in rows_sent:
        copy.wait()
    blocks = []
    block = table.at[pl.ds(pl.multiple_of(group_at * N_GRP, N_GRP), N_GRP), :]
    for k in range(1, PEERS):
        blocks.append(
            pltpu.make_async_remote_copy(block, block, blk_send.at[k], blk_recv.at[k], device_id=peer(k), device_id_type=MESH)
        )
    for copy in blocks:
        copy.start()
    for copy in moves[2 * per_chunk :]:
        copy.start()

    pl.loop(48, 64)(stencil)

    @pl.loop(0, S)
    def _(s):
        for c in range(8):
            cols = slice(c * 512, c * 512 + 512)
            both = jnp.concatenate([rec[s, :, cols], old[s, :, cols]], axis=0)
            stay = jnp.dot(keep, both, preferred_element_type=jnp.float32)
            base = padded[s, :, FACE + c * 512 : FACE + c * 512 + 512]
            new_fields[s, :, cols] = base + (STEP / 12.0) * stay

    for copy in blocks:
        copy.wait()
    id_col = column(ids[...])
    device = id_col >> 5
    row_of = ((device & 15) << 3) + (device >> 4)
    lanes = iota((SLOTS, 128), 1)
    row_hot = jnp.where(lanes == row_of, 1.0, 0.0)
    near = jnp.dot(row_hot, table[...], precision=lax.Precision.HIGHEST, preferred_element_type=jnp.float32)
    thick = jnp.sum(jnp.where(lanes == (id_col & 31), near, 0.0), axis=1, keepdims=True)
    inverse = 1.0 / thick

    for copy in slots:
        copy.wait()
    arrow = iota((2 * PEERS, 128), 0)
    acol = iota((2 * PEERS, 128), 1)
    here = (in_slot[...] == (acol & 31).astype(jnp.float32)) & ((acol >> 5) == (arrow & 1))
    place = jnp.where(here, 1.0, 0.0).T[0 : 2 * SLOTS, :]
    place = (place * jnp.concatenate([mask, mask], axis=0)).astype(jnp.bfloat16)

    for c, (s0, s1) in enumerate(CHUNKS):
        for copy in moves[c * per_chunk : (c + 1) * per_chunk]:
            copy.wait_recv()

        @pl.loop(s0, s1)
        def _(s):
            for n in range(4):
                moved = jnp.dot(place, in_msg[s, :, n * 512 : n * 512 + 512], preferred_element_type=jnp.float32)
                for h in range(2):
                    cols = slice(h * HALF + n * 512, h * HALF + n * 512 + 512)
                    tend = lap[s, :, cols] * thick + adv[s, :, cols] + react[s, :, cols] * inverse
                    new_tend[s, :, cols] = (tend * mask).astype(jnp.bfloat16)
                    part = new_fields[s, :, cols] + (STEP * 23.0 / 12.0) * tend
                    new_fields[s, :, cols] = part * mask + (STEP / 12.0) * moved[h * SLOTS : (h + 1) * SLOTS, :]

    for copy in halos:
        copy.wait_send()
    for copy in moves:
        copy.wait_send()


def local(fields, ghosts, velocity, rate, recent, older, destination, target, live, ids, sensor, flags):
    fields, ghosts, recent, older = (a.transpose(1, 0, 2) for a in (fields, ghosts, recent, older))
    vmem = pl.BlockSpec(memory_space=pltpu.VMEM)
    smem = pl.BlockSpec(memory_space=pltpu.SMEM)
    hbm = pl.BlockSpec(memory_space=pl.ANY)
    dma = pltpu.SemaphoreType.DMA
    f32, bf16 = jnp.float32, jnp.bfloat16
    new_fields, new_tend, filtered = pl.pallas_call(
        kernel,
        out_shape=(
            jax.ShapeDtypeStruct((S, SLOTS, CELLS), f32),
            jax.ShapeDtypeStruct((S, SLOTS, CELLS), bf16),
            jax.ShapeDtypeStruct((BZ, COLS), f32),
        ),
        in_specs=[hbm, hbm, vmem, smem, hbm, hbm, vmem, vmem, smem, vmem, hbm, smem],
        out_specs=(vmem, vmem, vmem),
        scratch_shapes=[
            pltpu.VMEM((S, SLOTS, CELLS + 2 * FACE), f32),
            pltpu.VMEM((S, SLOTS, 4 * FACE), f32),
            pltpu.VMEM((S, SLOTS, CELLS), bf16),
            pltpu.VMEM((S, SLOTS, CELLS), bf16),
            pltpu.VMEM((S, 2 * PEERS, HALF), bf16),
            pltpu.VMEM((S, 2 * PEERS, HALF), bf16),
            pltpu.VMEM((2 * PEERS, 128), f32),
            pltpu.VMEM((2 * PEERS, 128), f32),
            pltpu.VMEM((S, SLOTS, CELLS), f32),
            pltpu.VMEM((S, SLOTS, CELLS), f32),
            pltpu.VMEM((S, SLOTS, CELLS), f32),
            pltpu.VMEM((BZ, COLS), f32),
            pltpu.VMEM((BZ, COLS), bf16),
            pltpu.VMEM((BZ, COLS), bf16),
            pltpu.VMEM((BZ, COLS), bf16),
            pltpu.VMEM((BZ, COLS), bf16),
            pltpu.VMEM((N_GRP * PEERS, 128), f32),
            pltpu.VMEM((3, SLOTS, 128), f32),
            dma((7,)),
            dma((2,)),
            dma((2,)),
            dma((PEERS,)),
            dma((PEERS,)),
            dma((len(CHUNKS), PEERS)),
            dma((len(CHUNKS), PEERS)),
            dma((N_GRP,)),
            dma((N_GRP,)),
            dma((PEERS,)),
            dma((PEERS,)),
        ],
        compiler_params=pltpu.CompilerParams(
            collective_id=0, has_side_effects=True, vmem_limit_bytes=VMEM_LIMIT
        ),
        name="repartition_step",
    )(
        fields,
        ghosts,
        velocity,
        rate,
        recent,
        older,
        destination.reshape(1, SLOTS),
        target.reshape(1, SLOTS),
        live,
        ids.reshape(1, SLOTS),
        sensor,
        flags,
    )
    return new_fields.transpose(1, 0, 2), new_tend.transpose(1, 0, 2), filtered


VMEM_LIMIT = 44 << 20


def solution(mesh):
    tile = P(ALL_AXES, None, None)
    brick = P("pen", ("grp", "mig"))
    flat = P(ALL_AXES)
    return jax.shard_map(
        local,
        mesh=mesh,
        in_specs=(tile, tile, P(None, ALL_AXES), P(), tile, tile, flat, flat, flat, flat, brick, brick),
        out_specs=(tile, tile, brick),
        check_vma=False,
    )
```

time: 306 us -> 59.8 us (0.20); the launches traced: 301 us -> 59.4 us
  local copies, waits for them, and re-layouts: 135 us -> 17.1 us
  matrix products: 94.5 us -> 0 us
  Pallas kernels: 0 us -> 41 us
  blocking collectives: 36.7 us -> 0 us
  other arithmetic: 21.5 us -> 0 us
  starting transfers between devices: 10.3 us -> 0 us
    dot_general x15 -> x0, matrix products: 94.5 us -> none  [the longest x1 49.6 us: tendency(): jnp.einsum('sk,nkc->nsc', rate_matrix, fields * burning[:, None, :], prec...]
    unnamed x120 -> x23, local copies, waits for them, and re-layouts: 75.3 us -> 17.1 us
    pallas_call x0 -> x1, Pallas kernels: none -> 41 us  [local(): pl.pallas_call(kernel, out_shape=(jax.ShapeDtypeStruct((S, SLOTS, CELLS),...]
    reshape x14 -> x0, local copies, waits for them, and re-layouts: 38 us -> none  [the longest x6 37.5 us: outside(): return placed.reshape(lead, species, tile_cells)]
    all_gather x4 -> x0, blocking collectives: 36.7 us -> none  [all_blocks(): blocks = lax.all_gather(blocks, axes[k])]
    slice x14 -> x0, local copies, waits for them, and re-layouts: 20.5 us -> none  [the longest x6 17.4 us: inside(): return jnp.roll(fields, shift, axis=2) * interior.astype(jnp.float32)]
    convert_element_type x8 -> x0, other arithmetic: 6.62 us -> none  [the longest x1 1.98 us: local(): raw_sensor.astype(jnp.bfloat16)]
    all_to_all x2 -> x0, other arithmetic: 6.32 us -> none  [side_by_side(): lax.all_to_all(both, axis, split_axis=split_dim, concat_axis=concat_dim,...]
  transfers between devices with their start and end apart: 3 -> 0, of which waited for: 0 -> 0; matrix products, arithmetic and copies ran while one was open for 55% -> 0% of each run, Pallas kernels for 0% -> 0%
where the time goes in v1:
time: 59.8 us; the launch traced here: 59.4 us
  Pallas kernels  41 us (69%)
  local copies, waits for them, and re-layouts  17.1 us (29%)
  between operations  1.31 us (2%)
    pallas_call x1, Pallas kernels, local(): pl.pallas_call(kernel, out_shape=(jax.ShapeDtypeStruct((S, SLOTS, CELLS),...  41 us
    unnamed x23, local copies, waits for them, and re-layouts  17.1 us

profile of v1, /device:TPU:1, one launch (start us, length us, event | category | flops | bytes accessed | tf_op | source)
XLA Modules:
  0.0 59.4 jit_solution(12694031486224030378)
XLA Ops:
  1.3 0.0 copy-start
  1.3 1.7 %copy-done = bf16[32,9,4096]{2,0,1:T(8,128)(2,1)S(1)} copy-done((bf16[32,9,4096]{2,0,1:T(8,128)(2,1)S(1)}, bf16[32,9,4096]{2,0,1:T(8,128)(2,1)}, u32[]{:S(2)}) %copy-start) | copy-done | bytes 2359320
  2.9 0.0 copy-start.1
  2.9 1.7 %copy-done.1 = bf16[32,9,4096]{2,0,1:T(8,128)(2,1)S(1)} copy-done((bf16[32,9,4096]{2,0,1:T(8,128)(2,1)S(1)}, bf16[32,9,4096]{2,0,1:T(8,128)(2,1)}, u32[]{:S(2)}) %copy-start.1) | copy-done | bytes 2359320
  4.6 0.0 copy-start.2
  4.6 1.5 %copy-done.2 = f32[32,9,1536]{2,0,1:T(8,128)S(1)} copy-done((f32[32,9,1536]{2,0,1:T(8,128)S(1)}, f32[32,9,1536]{2,0,1:T(8,128)}, u32[]{:S(2)}) %copy-start.2) | copy-done | bytes 1769496
  6.1 0.0 copy-start.3
  6.1 1.0 %copy-done.3 = f32[32,4096]{1,0:T(8,128)S(1)} copy-done((f32[32,4096]{1,0:T(8,128)S(1)}, f32[32,4096]{1,0:T(8,128)}, u32[]{:S(2)}) %copy-start.3) | copy-done | bytes 524312
  7.1 0.0 copy-start.4
  7.1 0.7 %copy-done.4 = f32[9,9]{1,0:T(8,128)S(1)} copy-done((f32[9,9]{1,0:T(8,128)S(1)}, f32[9,9]{1,0:T(8,128)}, u32[]{:S(2)}) %copy-start.4) | copy-done | bytes 348
  7.8 0.0 copy-start.5
  7.8 0.7 %copy-done.5 = f32[3,32]{1,0:T(4,128)S(1)} copy-done((f32[3,32]{1,0:T(4,128)S(1)}, f32[3,32]{1,0:T(4,128)}, u32[]{:S(2)}) %copy-start.5) | copy-done | bytes 408
  8.5 0.0 copy-start.6
  8.5 0.7 %copy-done.6 = s32[2,16]{1,0:T(2,128)S(1)} copy-done((s32[2,16]{1,0:T(2,128)S(1)}, s32[2,16]{1,0:T(2,128)}, u32[]{:S(2)}) %copy-start.6) | copy-done | bytes 152
  9.2 0.0 copy-start.7
  9.2 0.7 %copy-done.7 = s32[32]{0:T(128)S(1)} copy-done((s32[32]{0:T(128)S(1)}, s32[32]{0:T(128)}, u32[]{:S(2)}) %copy-start.7) | copy-done | bytes 152
  9.8 0.0 copy-start.8
  9.8 0.7 %copy-done.8 = s32[32]{0:T(128)S(1)} copy-done((s32[32]{0:T(128)S(1)}, s32[32]{0:T(128)}, u32[]{:S(2)}) %copy-start.8) | copy-done | bytes 152
  10.5 0.0 copy-start.9
  10.5 0.7 %copy-done.9 = s32[32]{0:T(128)S(1)} copy-done((s32[32]{0:T(128)S(1)}, s32[32]{0:T(128)}, u32[]{:S(2)}) %copy-start.9) | copy-done | bytes 152
  11.2 41.0 %repartition_step.1 = (f32[9,32,4096]{2,1,0:T(8,128)}, bf16[9,32,4096]{2,1,0:T(8,128)(2,1)S(1)}, f32[32,4096]{1,0:T(8,128)S(1)}) custom-call(f32[9,32,4096]{2,1,0:T(8,128)} %bitcast.16, f32[9,32,1536]{2,1,0:T(8,128)S(1)} %bitcast.12, f32[3,32]{1,0:T(4,128)S(1)} %copy-done.5, f32[9,9]{1,0:T(8,128)S(1)} %copy-done.4, bf16[9,32,4096]{2,1,0:T(8,128)(2,1)S(1)} %bitcast.9, ...), custom_call_target="tpu_custom_call" | custom-call | tf_op jit(solution)/shard_map/repartition_step/pallas_call | solution.py:385
  52.2 5.0 %copy.19 = f32[32,9,4096]{2,0,1:T(8,128)} copy(f32[32,9,4096]{2,0,1:T(8,128)} %bitcast.17) | data formatting | bytes 9437184
  57.2 1.4 %copy.20 = bf16[32,9,4096]{2,0,1:T(8,128)(2,1)} copy(bf16[32,9,4096]{2,0,1:T(8,128)(2,1)S(1)} %bitcast.11) | data formatting | bytes 4718592
  58.6 0.8 %copy.21 = f32[32,4096]{1,0:T(8,128)} copy(f32[32,4096]{1,0:T(8,128)S(1)} %get-tuple-element.14) | data formatting | bytes 1048576
Async XLA Ops:
  1.3 1.7 %copy-start = (bf16[32,9,4096]{2,0,1:T(8,128)(2,1)S(1)}, bf16[32,9,4096]{2,0,1:T(8,128)(2,1)}, u32[]{:S(2)}) copy-start(bf16[32,9,4096]{2,0,1:T(8,128)(2,1)} %param.16) | copy-start | bytes 7077892
  2.9 1.7 %copy-start.1 = (bf16[32,9,4096]{2,0,1:T(8,128)(2,1)S(1)}, bf16[32,9,4096]{2,0,1:T(8,128)(2,1)}, u32[]{:S(2)}) copy-start(bf16[32,9,4096]{2,0,1:T(8,128)(2,1)} %param.17) | copy-start | bytes 7077892
  4.6 1.5 %copy-start.2 = (f32[32,9,1536]{2,0,1:T(8,128)S(1)}, f32[32,9,1536]{2,0,1:T(8,128)}, u32[]{:S(2)}) copy-start(f32[32,9,1536]{2,0,1:T(8,128)} %param.13) | copy-start | bytes 5308420
  6.1 1.0 %copy-start.3 = (f32[32,4096]{1,0:T(8,128)S(1)}, f32[32,4096]{1,0:T(8,128)}, u32[]{:S(2)}) copy-start(f32[32,4096]{1,0:T(8,128)} %sensor.1) | copy-start | bytes 1572868
  7.1 0.7 %copy-start.4 = (f32[9,9]{1,0:T(8,128)S(1)}, f32[9,9]{1,0:T(8,128)}, u32[]{:S(2)}) copy-start(f32[9,9]{1,0:T(8,128)} %rate.1) | copy-start | bytes 976
  7.8 0.7 %copy-start.5 = (f32[3,32]{1,0:T(4,128)S(1)}, f32[3,32]{1,0:T(4,128)}, u32[]{:S(2)}) copy-start(f32[3,32]{1,0:T(4,128)} %velocity.1) | copy-start | bytes 1156
  8.5 0.7 %copy-start.6 = (s32[2,16]{1,0:T(2,128)S(1)}, s32[2,16]{1,0:T(2,128)}, u32[]{:S(2)}) copy-start(s32[2,16]{1,0:T(2,128)} %flags.1) | copy-start | bytes 388
  9.2 0.7 %copy-start.7 = (s32[32]{0:T(128)S(1)}, s32[32]{0:T(128)}, u32[]{:S(2)}) copy-start(s32[32]{0:T(128)} %param.18) | copy-start | bytes 388
  9.8 0.7 %copy-start.8 = (s32[32]{0:T(128)S(1)}, s32[32]{0:T(128)}, u32[]{:S(2)}) copy-start(s32[32]{0:T(128)} %param.19) | copy-start | bytes 388
  10.5 0.7 %copy-start.9 = (s32[32]{0:T(128)S(1)}, s32[32]{0:T(128)}, u32[]{:S(2)}) copy-start(s32[32]{0:T(128)} %param.21) | copy-start | bytes 388

commit v2 on v1

--- a/solution.py
+++ b/solution.py
@@ -25,7 +25,9 @@
 STEP = 0.25
 SIGMA = BZ / 2.0
 GAUSS_TOTAL = sum(math.exp(-k * k / (2.0 * SIGMA * SIGMA)) for k in range(-BZ, BZ + 1))
-CHUNKS = ((0, 3), (3, 6), (6, 9))
+CHUNKS = ((0, 5), (5, 9))
+CUT = (0, 8, 36)
+LATER = 24
 
 
 def split(x):
@@ -46,16 +48,15 @@
 def kernel(
     fields,
     ghosts,
-    velocity,
-    rate,
+    velocity_hbm,
+    rate_hbm,
     recent,
     older,
-    destination,
-    target,
-    live,
-    ids,
+    destination_hbm,
+    target_hbm,
+    ids_hbm,
     sensor,
-    flags,
+    flags_hbm,
     new_fields,
     new_tend,
     filtered,
@@ -77,7 +78,17 @@
     nxt,
     table,
     vcol,
+    z_face,
+    z_terms,
+    z_place,
+    velocity,
+    rate,
+    destination,
+    target,
+    ids,
+    flags,
     local_sem,
+    small_sem,
     halo_send,
     halo_recv,
     slot_send,
@@ -88,6 +99,9 @@
     grp_recv,
     blk_send,
     blk_recv,
+    known,
+    mix_f,
+    mix,
 ):
     g, m, p = (lax.axis_index(a) for a in ALL_AXES)
     group_at = m * N_PEN + p
@@ -102,10 +116,9 @@
     in_slot[0:8, :] = jnp.full((8, 128), -1.0, jnp.float32)
 
     barrier = pltpu.get_barrier_semaphore()
-    for k in range(1, PEERS):
-        pl.semaphore_signal(barrier, inc=1, device_id=peer(k), device_id_type=MESH)
-    for k in range(1, N_GRP):
-        pl.semaphore_signal(barrier, inc=1, device_id=grp_peer(k), device_id_type=MESH)
+    near = [peer(1), peer(3), peer(4), peer(12), grp_peer(2), grp_peer(6), (g + 1 - 2 * lax.rem(g, 2), m, p)]
+    for device in near:
+        pl.semaphore_signal(barrier, inc=1, device_id=device, device_id_type=MESH)
 
     loads = [
         pltpu.make_async_copy(sensor, sens, local_sem.at[0]),
@@ -120,8 +133,19 @@
         ),
         pltpu.make_async_copy(ghosts.at[:, :, 2 * FACE : 6 * FACE], faces, local_sem.at[6]),
     ]
-    for copy in loads:
-        copy.start()
+    small = (
+        (flags_hbm, flags),
+        (destination_hbm, destination),
+        (target_hbm, target),
+        (velocity_hbm, velocity),
+        (ids_hbm, ids),
+        (rate_hbm, rate),
+    )
+    small = [pltpu.make_async_copy(a, b, small_sem.at[i]) for i, (a, b) in enumerate(small)]
+    for copy in loads[:1] + small + loads[1:]:
+        copy.start()
+    for copy in small:
+        copy.wait()
 
     dest = destination[...]
     slot = target[...]
@@ -140,17 +164,38 @@
     found = jnp.sum(jnp.where(hot32, slot_rows + 1.0, 0.0), axis=1, keepdims=True) - 1.0
     out_slot[...] = jnp.broadcast_to(found, (2 * PEERS, 128))
 
-    live_col = iota((SLOTS, 1), 0) < live[0]
-    mask = jnp.where(live_col, 1.0, 0.0)
     keep_row = iota((SLOTS, 2 * SLOTS), 0)
     keep_col = iota((SLOTS, 2 * SLOTS), 1)
     dest2 = jnp.broadcast_to(jnp.concatenate([dest] * 2, axis=1), keep_row.shape)
     slot2 = jnp.broadcast_to(jnp.concatenate([slot] * 2, axis=1), keep_row.shape)
     kept = (dest2 == group_at) & (slot2 == keep_row)
+    stays = jnp.sum(jnp.where(kept[:, 0:SLOTS], 1.0, 0.0), axis=1, keepdims=True)
     keep = jnp.where(kept, jnp.where(keep_col < SLOTS, -16.0, 5.0), 0.0).astype(jnp.bfloat16)
 
     for d in range(3):
         vcol[d] = jnp.broadcast_to(-0.5 * column(velocity[d : d + 1, :]), (SLOTS, 128))
+
+    z_place[...] = jnp.zeros((8, 512, FACE), jnp.bfloat16)
+    zy = iota((16, FACE), 0)
+    zc = iota((16, FACE), 1)
+    for part in range(4):
+        at_end = (zc & 15) == (0 if part < 2 else 15)
+        spot = jnp.where((zy == (zc >> 4)) & at_end, 1.0, 0.0).astype(jnp.bfloat16)
+        for x in range(8):
+            z_place[x, part * 128 + x * 16 : part * 128 + x * 16 + 16, :] = spot
+
+    at = iota((8, FACE), 1)
+    part = jnp.where(at < 80, 0, jnp.where(at < 160, 1, 2))
+    at = at - 80 * part
+    own = ((at & 7) == iota((8, FACE), 0)) & (part * 80 + at < 240)
+    for s in range(S):
+        row = jnp.zeros((8, FACE), jnp.float32)
+        for k in range(S):
+            row = jnp.where((at >> 3) == k, rate[s, k], row)
+        row = jnp.where(own, row, 0.0)
+        high = row.astype(jnp.bfloat16).astype(jnp.float32)
+        mix_f[s * 8 : s * 8 + 8, :] = jnp.where(part < 2, high, row - high)
+    mix[...] = mix_f[:, 0:240].astype(jnp.bfloat16)
 
     loads[0].wait()
     for t in range(2):
@@ -172,7 +217,7 @@
             both = jnp.concatenate([rec[s, :, low], old[s, :, low], rec[s, :, high], old[s, :, high]], axis=0)
             out_msg[s, :, low] = jnp.dot(select, both, preferred_element_type=jnp.float32).astype(jnp.bfloat16)
 
-    pl.semaphore_wait(barrier, PEERS - 1 + N_GRP - 1)
+    pl.semaphore_wait(barrier, len(near))
 
     halos = [
         pltpu.make_async_remote_copy(
@@ -184,6 +229,24 @@
     ]
     for copy in halos:
         copy.start()
+    loads[6].wait()
+    for h in range(2):
+        for f in range(2):
+            at = (2 + f) * FACE + h * 128
+            hi, lo = split(faces[:, :, at : at + 128].reshape(S * SLOTS, 128))
+            z_terms[h, :, f * 256 : f * 256 + 128] = hi
+            z_terms[h, :, f * 256 + 128 : f * 256 + 256] = lo
+
+    def z_plane(x):
+        spread = jnp.dot(z_terms[x // 8], z_place[x % 8], preferred_element_type=jnp.float32)
+        z_face[:, :, pl.ds(pl.multiple_of(x * FACE, FACE), FACE)] = spread.reshape(S, SLOTS, FACE)
+
+    for r in range(3):
+        for device in near:
+            pl.semaphore_signal(known.at[r], inc=1, device_id=device, device_id_type=MESH)
+        pl.loop((0, 5, 10)[r], (5, 10, 16)[r])(z_plane)
+        pl.semaphore_wait(known.at[r], len(near))
+
     slots = []
     for k in range(1, PEERS):
         rows = slice(2 * k, 2 * k + 2)
@@ -204,10 +267,12 @@
                 )
             )
     per_chunk = PEERS - 1
-    for copy in moves[: 2 * per_chunk]:
-        copy.start()
-
-    for copy in loads[3:]:
+    along_x = [copy for i, copy in enumerate(moves) if (i % per_chunk + 1) % N_PEN == 0]
+    rest = [copy for i, copy in enumerate(moves) if (i % per_chunk + 1) % N_PEN != 0]
+    for copy in along_x:
+        copy.start()
+
+    for copy in loads[3:6]:
         copy.wait()
     lane = iota((8, 128), 1)
     lane_z = lane & 15
@@ -221,8 +286,8 @@
         x = step % PLANES
         at_face = (x // 8) * 128
         in_face = (x % 8) * 16
-        idx_y = in_face + lane_z
-        idx_z = [in_face + t * 8 + (lane >> 4) for t in range(2)]
+        to_first = lax.rem(128 - in_face, 128)
+        to_last = lax.rem(240 - in_face, 128)
         vx, vy, vz = (vcol[d, rows, :] for d in range(3))
 
         def face(s, which):
@@ -233,41 +298,43 @@
 
         def put(ref, s, t, value):
             ref[s, rows, pl.ds(pl.multiple_of(x * FACE + t * 128, 128), 128)] = value
-
-        def pick(source, idx):
-            return jnp.take_along_axis(source, idx, axis=1)
 
         for s in range(S):
             now = [plane(s, 1, t) for t in range(2)]
             down = [pltpu.roll(v, 16, 1) for v in now]
             up = [pltpu.roll(v, 112, 1) for v in now]
             y_low = [
-                jnp.where(first_y, pick(face(s, 0), idx_y), down[0]),
+                jnp.where(first_y, pltpu.roll(face(s, 0), to_first, 1), down[0]),
                 jnp.where(first_y, down[0], down[1]),
             ]
             y_high = [
                 jnp.where(last_y, up[1], up[0]),
-                jnp.where(last_y, pick(face(s, 1), idx_y), up[1]),
+                jnp.where(last_y, pltpu.roll(face(s, 1), to_last, 1), up[1]),
             ]
             for t in range(2):
-                z_low = jnp.where(first_z, pick(face(s, 2), idx_z[t]), pltpu.roll(now[t], 1, 1))
-                z_high = jnp.where(last_z, pick(face(s, 3), idx_z[t]), pltpu.roll(now[t], 127, 1))
+                edge = z_face[s, rows, pl.ds(pl.multiple_of(x * FACE + t * 128, 128), 128)]
+                z_low = jnp.where(first_z, edge, pltpu.roll(now[t], 1, 1))
+                z_high = jnp.where(last_z, edge, pltpu.roll(now[t], 127, 1))
                 x_low = plane(s, 0, t)
                 x_high = plane(s, 2, t)
                 total = ((x_low + x_high) + (y_low[t] + y_high[t])) + (z_low + z_high)
-                put(lap, s, t, VISCOUS * (total - 6.0 * now[t]))
+                put(lap, s, t, total - 6.0 * now[t])
                 put(adv, s, t, vx * (x_high - x_low) + vy * (y_high[t] - y_low[t]) + vz * (z_high - z_low))
-        for t in range(2):
-            f = [plane(s, 1, t) for s in range(S)]
-            burning = f[0] * f[1]
-            f = [v * burning for v in f]
-            for s in range(S):
-                total = rate[s, 0] * f[0]
-                for k in range(1, S):
-                    total = total + rate[s, k] * f[k]
-                put(react, s, t, total)
-
-    pl.loop(0, 32)(stencil)
+        here = pl.ds(pl.multiple_of((x + 1) * FACE, FACE), FACE)
+        f = [padded[s, rows, here] for s in range(S)]
+        burning = f[0] * f[1]
+        f = jnp.concatenate([v * burning for v in f] + [jnp.zeros_like(burning)], axis=0)
+        hi, lo = split(f)
+        mixed = jnp.dot(mix[...], jnp.concatenate([hi, lo, hi], axis=0), preferred_element_type=jnp.float32)
+        for s in range(S):
+            react[s, rows, pl.ds(pl.multiple_of(x * FACE, FACE), FACE)] = mixed[s * 8 : s * 8 + 8, :]
+
+    pl.loop(0, CUT[0])(stencil)
+    for copy in halos:
+        copy.wait_send()
+    for copy in rest[:LATER]:
+        copy.start()
+    pl.loop(CUT[0], CUT[1])(stencil)
 
     for copy in halos:
         copy.wait_recv()
@@ -309,7 +376,7 @@
     for copy in rows_sent:
         copy.start()
 
-    pl.loop(32, 48)(stencil)
+    pl.loop(CUT[1], CUT[2])(stencil)
 
     for copy in rows_sent:
         copy.wait()
@@ -321,10 +388,10 @@
         )
     for copy in blocks:
         copy.start()
-    for copy in moves[2 * per_chunk :]:
-        copy.start()
-
-    pl.loop(48, 64)(stencil)
+    for copy in rest[LATER:]:
+        copy.start()
+
+    pl.loop(CUT[2], 64)(stencil)
 
     @pl.loop(0, S)
     def _(s):
@@ -345,6 +412,7 @@
     near = jnp.dot(row_hot, table[...], precision=lax.Precision.HIGHEST, preferred_element_type=jnp.float32)
     thick = jnp.sum(jnp.where(lanes == (id_col & 31), near, 0.0), axis=1, keepdims=True)
     inverse = 1.0 / thick
+    spreading = VISCOUS * thick
 
     for copy in slots:
         copy.wait()
@@ -352,7 +420,8 @@
     acol = iota((2 * PEERS, 128), 1)
     here = (in_slot[...] == (acol & 31).astype(jnp.float32)) & ((acol >> 5) == (arrow & 1))
     place = jnp.where(here, 1.0, 0.0).T[0 : 2 * SLOTS, :]
-    place = (place * jnp.concatenate([mask, mask], axis=0)).astype(jnp.bfloat16)
+    mask = stays + jnp.sum(place[0:SLOTS, :], axis=1, keepdims=True)
+    place = place.astype(jnp.bfloat16)
 
     for c, (s0, s1) in enumerate(CHUNKS):
         for copy in moves[c * per_chunk : (c + 1) * per_chunk]:
@@ -364,22 +433,22 @@
                 moved = jnp.dot(place, in_msg[s, :, n * 512 : n * 512 + 512], preferred_element_type=jnp.float32)
                 for h in range(2):
                     cols = slice(h * HALF + n * 512, h * HALF + n * 512 + 512)
-                    tend = lap[s, :, cols] * thick + adv[s, :, cols] + react[s, :, cols] * inverse
+                    tend = lap[s, :, cols] * spreading + adv[s, :, cols] + react[s, :, cols] * inverse
                     new_tend[s, :, cols] = (tend * mask).astype(jnp.bfloat16)
                     part = new_fields[s, :, cols] + (STEP * 23.0 / 12.0) * tend
                     new_fields[s, :, cols] = part * mask + (STEP / 12.0) * moved[h * SLOTS : (h + 1) * SLOTS, :]
 
-    for copy in halos:
-        copy.wait_send()
     for copy in moves:
         copy.wait_send()
 
 
 def local(fields, ghosts, velocity, rate, recent, older, destination, target, live, ids, sensor, flags):
     fields, ghosts, recent, older = (a.transpose(1, 0, 2) for a in (fields, ghosts, recent, older))
+    rows = (a.reshape(1, SLOTS) for a in (destination, target, ids))
+    destination, target, ids = rows
+    args = (fields, ghosts, velocity, rate, recent, older, destination, target, ids, sensor, flags)
     vmem = pl.BlockSpec(memory_space=pltpu.VMEM)
-    smem = pl.BlockSpec(memory_space=pltpu.SMEM)
-    hbm = pl.BlockSpec(memory_space=pl.ANY)
+    hbm = pl.BlockSpec(memory_space=pltpu.HBM)
     dma = pltpu.SemaphoreType.DMA
     f32, bf16 = jnp.float32, jnp.bfloat16
     new_fields, new_tend, filtered = pl.pallas_call(
@@ -389,7 +458,7 @@
             jax.ShapeDtypeStruct((S, SLOTS, CELLS), bf16),
             jax.ShapeDtypeStruct((BZ, COLS), f32),
         ),
-        in_specs=[hbm, hbm, vmem, smem, hbm, hbm, vmem, vmem, smem, vmem, hbm, smem],
+        in_specs=[hbm] * 11,
         out_specs=(vmem, vmem, vmem),
         scratch_shapes=[
             pltpu.VMEM((S, SLOTS, CELLS + 2 * FACE), f32),
@@ -410,6 +479,16 @@
             pltpu.VMEM((BZ, COLS), bf16),
             pltpu.VMEM((N_GRP * PEERS, 128), f32),
             pltpu.VMEM((3, SLOTS, 128), f32),
+            pltpu.VMEM((S, SLOTS, CELLS), f32),
+            pltpu.VMEM((2, S * SLOTS, 512), bf16),
+            pltpu.VMEM((8, 512, FACE), bf16),
+            pltpu.VMEM((3, SLOTS), f32),
+            pltpu.SMEM((S, S), f32),
+            pltpu.VMEM((1, SLOTS), jnp.int32),
+            pltpu.VMEM((1, SLOTS), jnp.int32),
+            pltpu.VMEM((1, SLOTS), jnp.int32),
+            pltpu.SMEM((2, 16), jnp.int32),
+            dma((7,)),
             dma((7,)),
             dma((2,)),
             dma((2,)),
@@ -421,29 +500,19 @@
             dma((N_GRP,)),
             dma((PEERS,)),
             dma((PEERS,)),
+            pltpu.SemaphoreType.REGULAR((3,)),
+            pltpu.VMEM((S * 8, FACE), f32),
+            pltpu.VMEM((S * 8, 240), bf16),
         ],
         compiler_params=pltpu.CompilerParams(
             collective_id=0, has_side_effects=True, vmem_limit_bytes=VMEM_LIMIT
         ),
         name="repartition_step",
-    )(
-        fields,
-        ghosts,
-        velocity,
-        rate,
-        recent,
-        older,
-        destination.reshape(1, SLOTS),
-        target.reshape(1, SLOTS),
-        live,
-        ids.reshape(1, SLOTS),
-        sensor,
-        flags,
-    )
+    )(*(pltpu.with_memory_space_constraint(a, pltpu.HBM) for a in args))
     return new_fields.transpose(1, 0, 2), new_tend.transpose(1, 0, 2), filtered
 
 
-VMEM_LIMIT = 44 << 20
+VMEM_LIMIT = 40 << 20
 
 
 def solution(mesh):

time: 59.8 us -> 42.1 us (0.70)
  local copies, waits for them, and re-layouts: 17.1 us -> 4.39 us
  Pallas kernels: 41 us -> 36.3 us
  between operations: 1.31 us -> 0.64 us
    unnamed x23 -> x3, local copies, waits for them, and re-layouts: 17.1 us -> 4.39 us
    pallas_call x1, Pallas kernels: 41 us -> 36.3 us  [local(): pl.pallas_call(kernel, out_shape=(jax.ShapeDtypeStruct((S, SLOTS, CELLS),...]
where the time goes in v2:
time: 42.1 us; the launch traced here: 41.4 us
  Pallas kernels  36.3 us (86%)
  local copies, waits for them, and re-layouts  4.39 us (10%)
  between operations  0.64 us (2%)
    pallas_call x1, Pallas kernels, local(): pl.pallas_call(kernel, out_shape=(jax.ShapeDtypeStruct((S, SLOTS, CELLS),...  36.3 us
    unnamed x3, local copies, waits for them, and re-layouts  4.39 us

profile of v2, /device:TPU:1, one launch (start us, length us, event | category | flops | bytes accessed | tf_op | source)
XLA Modules:
  0.0 41.4 jit_solution(1912868726442863335)
XLA Ops:
  0.6 36.3 %repartition_step.1 = (f32[9,32,4096]{2,1,0:T(8,128)S(1)}, bf16[9,32,4096]{2,1,0:T(8,128)(2,1)S(1)}, f32[32,4096]{1,0:T(8,128)S(1)}) custom-call(f32[9,32,4096]{2,1,0:T(8,128)} %bitcast.11, f32[9,32,1536]{2,1,0:T(8,128)} %bitcast.14, f32[3,32]{1,0:T(4,128)} %velocity_hbm.1, f32[9,9]{1,0:T(8,128)} %rate_hbm.1, bf16[9,32,4096]{2,1,0:T(8,128)(2,1)} %bitcast.12, ...), custom_call_target="tpu_custom_call" | custom-call | tf_op jit(solution)/shard_map/repartition_step/pallas_call | solution.py:454
  37.0 2.2 %copy.17 = f32[32,9,4096]{2,0,1:T(8,128)} copy(f32[32,9,4096]{2,0,1:T(8,128)S(1)} %bitcast.9) | data formatting | bytes 9437184
  39.2 1.4 %copy.18 = bf16[32,9,4096]{2,0,1:T(8,128)(2,1)} copy(bf16[32,9,4096]{2,0,1:T(8,128)(2,1)S(1)} %bitcast.10) | data formatting | bytes 4718592
  40.6 0.8 %copy.19 = f32[32,4096]{1,0:T(8,128)} copy(f32[32,4096]{1,0:T(8,128)S(1)} %get-tuple-element.14) | data formatting | bytes 1048576

commit v3 on v2

--- a/solution.py
+++ b/solution.py
@@ -209,14 +209,14 @@
     loads[1].wait()
     loads[2].wait()
 
-    @pl.loop(0, S)
-    def _(s):
+    def messages(s):
         for c in range(4):
             low = slice(c * 512, c * 512 + 512)
             high = slice(HALF + c * 512, HALF + c * 512 + 512)
             both = jnp.concatenate([rec[s, :, low], old[s, :, low], rec[s, :, high], old[s, :, high]], axis=0)
             out_msg[s, :, low] = jnp.dot(select, both, preferred_element_type=jnp.float32).astype(jnp.bfloat16)
 
+    pl.loop(0, 3)(messages)
     pl.semaphore_wait(barrier, len(near))
 
     halos = [
@@ -244,6 +244,7 @@
     for r in range(3):
         for device in near:
             pl.semaphore_signal(known.at[r], inc=1, device_id=device, device_id_type=MESH)
+        pl.loop((3, 5, 7)[r], (5, 7, 9)[r])(messages)
         pl.loop((0, 5, 10)[r], (5, 10, 16)[r])(z_plane)
         pl.semaphore_wait(known.at[r], len(near))
 

time: 42.1 us -> 41.7 us (level)
  no operation moved by 1% of the time
where the time goes in v3:
time: 41.7 us; the launch traced here: 41.3 us
  Pallas kernels  36.3 us (87%)
  local copies, waits for them, and re-layouts  4.39 us (11%)
  between operations  0.64 us (2%)
    pallas_call x1, Pallas kernels, local(): pl.pallas_call(kernel, out_shape=(jax.ShapeDtypeStruct((S, SLOTS, CELLS),...  36.3 us
    unnamed x3, local copies, waits for them, and re-layouts  4.39 us

profile of v3, /device:TPU:1, one launch (start us, length us, event | category | flops | bytes accessed | tf_op | source)
XLA Modules:
  0.0 41.3 jit_solution(11532287868795924601)
XLA Ops:
  0.6 36.3 %repartition_step.1 = (f32[9,32,4096]{2,1,0:T(8,128)S(1)}, bf16[9,32,4096]{2,1,0:T(8,128)(2,1)S(1)}, f32[32,4096]{1,0:T(8,128)S(1)}) custom-call(f32[9,32,4096]{2,1,0:T(8,128)} %bitcast.11, f32[9,32,1536]{2,1,0:T(8,128)} %bitcast.14, f32[3,32]{1,0:T(4,128)} %velocity_hbm.1, f32[9,9]{1,0:T(8,128)} %rate_hbm.1, bf16[9,32,4096]{2,1,0:T(8,128)(2,1)} %bitcast.12, ...), custom_call_target="tpu_custom_call" | custom-call | tf_op jit(solution)/shard_map/repartition_step/pallas_call | solution.py:455
  36.9 2.2 %copy.17 = f32[32,9,4096]{2,0,1:T(8,128)} copy(f32[32,9,4096]{2,0,1:T(8,128)S(1)} %bitcast.9) | data formatting | bytes 9437184
  39.1 1.4 %copy.18 = bf16[32,9,4096]{2,0,1:T(8,128)(2,1)} copy(bf16[32,9,4096]{2,0,1:T(8,128)(2,1)S(1)} %bitcast.10) | data formatting | bytes 4718592
  40.5 0.8 %copy.19 = f32[32,4096]{1,0:T(8,128)} copy(f32[32,4096]{1,0:T(8,128)S(1)} %get-tuple-element.14) | data formatting | bytes 1048576
